TPU v7x, 32 devices: a whole 2x2x4 slice. The times are simulated.
32 devices in a mesh: grp: 2 (over y), row: 4 (over z), col: 2 (over x), rep: 2 (over core).
Axes of the slice: x: 2, y: 2, z: 4, core: 2. Of those that a mesh axis runs over, the one named last changes fastest.
Arguments:
- shard_rows: bfloat16 [11520, 512], P(('grp', 'row', 'col', 'rep')), parts along dimension 0, may hold values from -24 to 24
- row_position: int32 [11520], P(('grp', 'row', 'col', 'rep')), parts along dimension 0, may hold values from 0 to 3071, as said below
- shard_count: int32 [32], P(('grp', 'row', 'col', 'rep')), parts along dimension 0, may hold values from 1 to 360, as said below
Outputs:
- max_similarity: float32 [6144], P(('grp', 'row', 'col', 'rep')), parts along dimension 0
There are 2 independent parts, one for each index of `grp`. A program takes and returns all parts, laid end to end along the dimension named above; each array names one. Nothing has to cross between parts.
Inputs may be any that keep to these rules, and one draw needn't show every extreme that they name: `row_position`: row j of shard s is used when j < shard_count[s]; the used rows of all shards hold every position 0 to 3071 once, unused rows hold arbitrary positions. At most 24 used rows of one shard have positions in one aligned run of 192 positions, and some shard reaches 24. `shard_count`: the counts sum to 3072.
All inputs are finite; a program needn't handle non-finite values.
Results may differ from a plain program's by a relative error of at most 0.00063.
Values may be sent and summed in bfloat16 or wider, within the bound.
A program may use at most 64 MiB of HBM per device.

v0:
```python
import math
import jax
import jax.numpy as jnp
from jax import lax
from jax.sharding import PartitionSpec as P

OWN = 192


def normalize(owned_rows):
    widened = owned_rows.astype(jnp.float32)
    return (widened / jnp.sqrt(jnp.sum(widened * widened, 1, keepdims=True) + 1e-06)).astype(
        jnp.bfloat16
    )


def body(shard_rows, row_position, shard_count):
    row_devices = lax.axis_size("row")
    cross_devices = lax.axis_size(("col", "rep"))
    all_shards = row_devices * cross_devices
    per_owner = OWN
    owner_load = max(1, per_owner // all_shards)
    slot_count = 2 * owner_load
    block_rows = per_owner * cross_devices
    capacity, feature = shard_rows.shape
    row_place = lax.axis_index("row")
    cross_place = lax.axis_index(("col", "rep"))
    is_used = jnp.arange(capacity) < shard_count[0]
    position = jnp.where(is_used, row_position, 0)
    owner_first = position // per_owner
    one_hot = jnp.logical_and(
        owner_first[:, None] == jnp.arange(all_shards)[None, :], is_used[:, None]
    ).astype(jnp.int32)
    ranking = jnp.sum(jnp.cumsum(one_hot, 0) * one_hot, 1) - 1
    target = jnp.where(is_used, owner_first * slot_count + ranking, all_shards * slot_count)
    packed = (
        jnp.zeros((all_shards * slot_count, feature), shard_rows.dtype)
        .at[target]
        .set(shard_rows, mode="drop")
    )
    placed = (
        jnp.full((all_shards * slot_count,), -1, jnp.int32).at[target].set(position, mode="drop")
    )
    first_packed = packed.reshape(row_devices, cross_devices, slot_count, feature)
    first_placed = placed.reshape(row_devices, cross_devices, slot_count)
    own_offset = row_place * block_rows + cross_place * per_owner
    received = (
        lax.all_to_all(
            lax.all_to_all(first_packed, "row", split_axis=0, concat_axis=0, tiled=True),
            ("col", "rep"),
            split_axis=1,
            concat_axis=1,
            tiled=True,
        ),
        lax.all_to_all(
            lax.all_to_all(first_placed, "row", split_axis=0, concat_axis=0, tiled=True),
            ("col", "rep"),
            split_axis=1,
            concat_axis=1,
            tiled=True,
        ),
    )
    flat_rows = received[0].reshape(-1, feature)
    flat_places = received[1].reshape(-1)
    local_index = jnp.where(flat_places >= 0, flat_places - own_offset, per_owner)
    owned_rows = (
        jnp.zeros((per_owner, feature), flat_rows.dtype).at[local_index].set(flat_rows, mode="drop")
    )
    row_owned = normalize(owned_rows)
    row_block = lax.all_gather(row_owned, ("col", "rep"), axis=0, tiled=True)
    column_index = jnp.arange(block_rows)
    column_block = lax.all_gather(row_owned, "row", axis=0, tiled=True)
    column_places = (
        column_index // per_owner * block_rows + cross_place * per_owner + column_index % per_owner
    )
    row_step = math.gcd(block_rows, 512)
    column_step = math.gcd(block_rows, 1024)

    def row_maxima(inputs):
        row_tile, row_start = inputs
        row_global = row_place * block_rows + row_start + jnp.arange(row_step)
        running = jnp.full((row_step,), -4.0, jnp.float32)
        for column_turn in range(block_rows // column_step):
            column_tile = column_block[column_turn * column_step : (column_turn + 1) * column_step]
            scores = jnp.einsum(
                "rd,cd->rc", row_tile, column_tile, preferred_element_type=jnp.float32
            )
            column_global = column_places[
                column_turn * column_step : (column_turn + 1) * column_step
            ]
            scores = jnp.where(row_global[:, None] == column_global[None, :], -4.0, scores)
            running = jnp.maximum(running, jnp.max(scores, 1))
        return running

    starts = jnp.arange(block_rows // row_step, dtype=jnp.int32) * row_step
    maxima = lax.map(row_maxima, (row_block.reshape(-1, row_step, feature), starts)).reshape(
        block_rows
    )
    combined = lax.pmax(maxima, ("col", "rep"))
    return lax.dynamic_slice_in_dim(combined, cross_place * per_owner, per_owner)


def solution(mesh):
    return jax.shard_map(
        body,
        mesh=mesh,
        in_specs=(
            P(("grp", "row", "col", "rep"), None),
            P(("grp", "row", "col", "rep")),
            P(("grp", "row", "col", "rep")),
        ),
        out_specs=P(("grp", "row", "col", "rep")),
        check_vma=False,
    )
```

profile of v0, /device:TPU:0, one launch (start us, length us, event | category | flops | bytes accessed | tf_op | source)
XLA Modules:
  0.0 92.6 jit_solution(1535740901777857113)
XLA Ops:
  0.7 0.7 copy-done
  1.4 0.9 reduce-window.6
  2.6 2.9 %scatter_custom_fusion = s32[384]{0:T(512)S(1)} fusion(s32[360]{0:T(512)S(1)} %compare_select_fusion.1, s32[360]{0:T(512)S(1)} %get-tuple-element.104, s32[]{:T(128)} %constant.84.clone.1), kind=kCustom, calls=%fused_computation.67 | custom fusion | bytes 1540 | tf_op jit(solution)/shard_map/scatter | solution.py:42
  5.5 0.7 reshape.115
  6.2 6.3 %all-to-all-start = ((s32[4,4,24]{2,1,0:T(4,128)}), s32[4,4,24]{2,1,0:T(4,128)S(1)}, u32[]{:S(2)}, u32[]{:S(2)}) async-start(s32[4,4,24]{2,1,0:T(4,128)} %reshape.115), calls=%async_computation | async-start | bytes 16384 | tf_op jit(solution)/shard_map/all_to_all | solution.py:56
  12.6 3.0 %scatter_custom_fusion.1 = bf16[384,512]{1,0:T(8,128)(2,1)} fusion(s32[360]{0:T(512)S(1)} %compare_select_fusion.1, bf16[360,512]{1,0:T(8,128)(2,1)} %param.5, bf16[]{:T(256)} %constant.83.clone.1), kind=kCustom, calls=%fused_computation.27 | custom fusion | bytes 393728 | tf_op jit(solution)/shard_map/scatter | solution.py:39
  15.6 2.6 %all-to-all-done = s32[4,4,24]{2,1,0:T(4,128)S(1)} async-done(((s32[4,4,24]{2,1,0:T(4,128)}), s32[4,4,24]{2,1,0:T(4,128)S(1)}, u32[]{:S(2)}, u32[]{:S(2)}) %all-to-all-start) | async-done | bytes 1568 | tf_op jit(solution)/shard_map/all_to_all | solution.py:56
  18.2 3.5 %all-to-all-start.2 = ((bf16[4,4,24,512]{3,2,1,0:T(8,128)(2,1)}), bf16[4,4,24,512]{3,2,1,0:T(8,128)(2,1)S(1)}, u32[]{:S(2)}, u32[]{:S(2)}) async-start(bf16[4,4,24,512]{3,2,1,0:T(8,128)(2,1)} %bitcast.5), calls=%async_computation.2 | async-start | bytes 786432 | tf_op jit(solution)/shard_map/all_to_all | solution.py:49
  21.6 0.6 copy.17
  22.2 9.9 %all-to-all-done.2 = bf16[4,4,24,512]{3,2,1,0:T(8,128)(2,1)S(1)} async-done(((bf16[4,4,24,512]{3,2,1,0:T(8,128)(2,1)}), bf16[4,4,24,512]{3,2,1,0:T(8,128)(2,1)S(1)}, u32[]{:S(2)}, u32[]{:S(2)}) %all-to-all-start.2) | async-done | bytes 393248 | tf_op jit(solution)/shard_map/all_to_all | solution.py:49
  32.1 3.2 %all-to-all-start.1 = ((s32[4,4,24]{2,0,1:T(4,128)}), s32[4,4,24]{2,0,1:T(4,128)S(1)}, u32[]{:S(2)}, u32[]{:S(2)}) async-start(s32[4,4,24]{2,0,1:T(4,128)} %copy.17), calls=%async_computation.1 | async-start | bytes 16384 | tf_op jit(solution)/shard_map/all_to_all | solution.py:55
  35.4 0.8 copy.19
  36.2 3.0 %all-to-all-done.1 = s32[4,4,24]{2,0,1:T(4,128)S(1)} async-done(((s32[4,4,24]{2,0,1:T(4,128)}), s32[4,4,24]{2,0,1:T(4,128)S(1)}, u32[]{:S(2)}, u32[]{:S(2)}) %all-to-all-start.1) | async-done | bytes 1568 | tf_op jit(solution)/shard_map/all_to_all | solution.py:55
  39.1 3.5 %all-to-all-start.3 = ((bf16[4,4,24,512]{3,2,0,1:T(8,128)(2,1)}), bf16[4,4,24,512]{3,2,0,1:T(8,128)(2,1)S(1)}, u32[]{:S(2)}, u32[]{:S(2)}) async-start(bf16[4,4,24,512]{3,2,0,1:T(8,128)(2,1)} %copy.19), calls=%async_computation.3 | async-start | bytes 786432 | tf_op jit(solution)/shard_map/all_to_all | solution.py:48
  42.7 7.3 %all-to-all-done.3 = bf16[4,4,24,512]{3,2,0,1:T(8,128)(2,1)S(1)} async-done(((bf16[4,4,24,512]{3,2,0,1:T(8,128)(2,1)}), bf16[4,4,24,512]{3,2,0,1:T(8,128)(2,1)S(1)}, u32[]{:S(2)}, u32[]{:S(2)}) %all-to-all-start.3) | async-done | bytes 393248 | tf_op jit(solution)/shard_map/all_to_all | solution.py:48
  50.0 2.0 %scatter_custom_fusion.2 = bf16[192,512]{1,0:T(8,128)(2,1)S(1)} fusion(s32[384]{0:T(512)S(1)} %fusion.35, bf16[384,512]{1,0:T(8,128)(2,1)S(1)} %bitcast.40, bf16[]{:T(256)} %constant.83.clone.1), kind=kCustom, calls=%fused_computation.29 | custom fusion | bytes 196610 | tf_op jit(solution)/shard_map/scatter | solution.py:67
  52.3 18.0 %all_gather.7 = bf16[768,512]{1,0:T(8,128)(2,1)S(1)} all-gather(bf16[192,512]{1,0:T(8,128)(2,1)S(1)} %fusion.16), channel_id=1, replica_groups=mesh['grp'=2,'row'=4,'col'=2,'rep'=2] {'row'}, dimensions={0}, use_global_device_ids=true | all-gather | bytes 983040 | tf_op jit(solution)/shard_map/all_gather | solution.py:72
  70.3 7.5 %all_gather.6 = bf16[768,512]{1,0:T(8,128)(2,1)S(1)} all-gather(bf16[192,512]{1,0:T(8,128)(2,1)S(1)} %fusion.16), channel_id=1, replica_groups=mesh['grp'=2,'row'=4,'col'=2,'rep'=2] {'col','rep'}, dimensions={0}, use_global_device_ids=true | all-gather | bytes 983040 | tf_op jit(solution)/shard_map/all_gather | solution.py:70
  77.8 6.9 %while.12 = (s32[]{:T(128)}, f32[3,256]{1,0:T(4,128)S(1)}, s32[3]{0:T(128)S(1)}, s32[]{:T(128)}, s32[768]{0:T(1024)S(1)}, /*index=5*/bf16[3,256,512]{2,1,0:T(8,1...) while((s32[]{:T(128)}, f32[3,256]{1,0:T(4,128)S(1)}, s32[3]{0:T(128)S(1)}, s32[]{:T(128)}, ...), condition=%wide.region_11.12_spmd, body=%wide.region_7.11_spmd.sunk | while | flops 201916672 | bytes 1595529 | solution.py:96
  77.8 0.7 dynamic_slice.35
  79.1 0.3 fusion.58
  79.4 0.3 fusion.57
  79.7 0.3 fusion.56
  80.1 0.7 dynamic_slice.35
  81.4 0.3 fusion.58
  81.7 0.3 fusion.57
  82.0 0.3 fusion.56
  82.3 0.7 dynamic_slice.35
  83.7 0.3 fusion.58
  84.3 0.3 fusion.56
  84.6 7.3 %pmax.7 = f32[768]{0:T(1024)S(1)} all-reduce(f32[768]{0:T(1024)S(1)} %reshape.119), channel_id=1, replica_groups=mesh['grp'=2,'row'=4,'col'=2,'rep'=2] {'col','rep'}, use_global_device_ids=true, to_apply=%region_12.13 | all-reduce | flops 768 | bytes 6144 | tf_op jit(solution)/shard_map/pmax | solution.py:99
  91.9 0.6 dynamic_slice.15
  (32 shorter events, 1.3 us)
Async XLA Ops:
  0.7 0.7 copy-start
  6.2 11.9 %all-to-all-start = ((s32[4,4,24]{2,1,0:T(4,128)}), s32[4,4,24]{2,1,0:T(4,128)S(1)}, u32[]{:S(2)}, u32[]{:S(2)}) async-start(s32[4,4,24]{2,1,0:T(4,128)} %reshape.115), calls=%async_computation | async-start | bytes 16384 | tf_op jit(solution)/shard_map/all_to_all | solution.py:56
  18.2 14.0 %all-to-all-start.2 = ((bf16[4,4,24,512]{3,2,1,0:T(8,128)(2,1)}), bf16[4,4,24,512]{3,2,1,0:T(8,128)(2,1)S(1)}, u32[]{:S(2)}, u32[]{:S(2)}) async-start(bf16[4,4,24,512]{3,2,1,0:T(8,128)(2,1)} %bitcast.5), calls=%async_computation.2 | async-start | bytes 786432 | tf_op jit(solution)/shard_map/all_to_all | solution.py:49
  32.1 7.0 %all-to-all-start.1 = ((s32[4,4,24]{2,0,1:T(4,128)}), s32[4,4,24]{2,0,1:T(4,128)S(1)}, u32[]{:S(2)}, u32[]{:S(2)}) async-start(s32[4,4,24]{2,0,1:T(4,128)} %copy.17), calls=%async_computation.1 | async-start | bytes 16384 | tf_op jit(solution)/shard_map/all_to_all | solution.py:55
  39.1 10.9 %all-to-all-start.3 = ((bf16[4,4,24,512]{3,2,0,1:T(8,128)(2,1)}), bf16[4,4,24,512]{3,2,0,1:T(8,128)(2,1)S(1)}, u32[]{:S(2)}, u32[]{:S(2)}) async-start(bf16[4,4,24,512]{3,2,0,1:T(8,128)(2,1)} %copy.19), calls=%async_computation.3 | async-start | bytes 786432 | tf_op jit(solution)/shard_map/all_to_all | solution.py:48
where the time goes:
time: 93.1 us; the launch traced here: 92.6 us
  blocking collectives  32.8 us (35%)
  waiting for transfers between devices  22.7 us (24%)
  starting transfers between devices  16.5 us (18%)
  local copies, waits for them, and re-layouts  13.7 us (15%)
  matrix products  2.53 us (3%)
  loops' own time  2.18 us (2%)
  other arithmetic  1.38 us (1%)
    all_gather x1, blocking collectives, body(): column_block = lax.all_gather(row_owned, 'row', axis=0, tiled=True)  18 us
    all_to_all x1, waiting for transfers between devices, body(): lax.all_to_all(first_packed, 'row', split_axis=0, concat_axis=0, tiled=True)  9.87 us
    all_gather x1, blocking collectives, body(): row_block = lax.all_gather(row_owned, ('col', 'rep'), axis=0, tiled=True)  7.46 us
    pmax x1, blocking collectives, body(): combined = lax.pmax(maxima, ('col', 'rep'))  7.28 us
    all_to_all x1, waiting for transfers between devices, body(): lax.all_to_all(lax.all_to_all(first_packed, 'row', split_axis=0, concat_a...  7.27 us
    all_to_all x1, starting transfers between devices, body(): lax.all_to_all(first_placed, 'row', split_axis=0, concat_axis=0, tiled=True)  6.32 us
    all_to_all x1, starting transfers between devices, body(): lax.all_to_all(lax.all_to_all(first_packed, 'row', split_axis=0, concat_a...  3.46 us
    all_to_all x1, starting transfers between devices, body(): lax.all_to_all(first_packed, 'row', split_axis=0, concat_axis=0, tiled=True)  3.46 us
  transfers between devices with their start and end apart: 4, of which 4 were waited for; matrix products, arithmetic and copies ran while one was open for 5% of the time, Pallas kernels for 0%

commit v1 on v0

--- a/solution.py
+++ b/solution.py
@@ -5,6 +5,22 @@
 from jax.sharding import PartitionSpec as P
 
 OWN = 192
+
+
+def fix_digits(original):
+    r1, big = (lax.axis_size("row"), lax.axis_index("row"))
+    block_next = original.shape[0] // r1
+    plain = list(original.shape)
+    plain[0] = block_next
+    back = plain[0]
+    plain[0] = back * r1
+    y_new = jnp.zeros(plain, original.dtype)
+    for it in range(r1):
+        work_now = lax.dynamic_slice_in_dim(original, (big ^ it) * block_next, block_next, axis=0)
+        if it:
+            work_now = lax.ppermute(work_now, "row", list(map(lambda ii: (ii, ii ^ it), range(r1))))
+        y_new = lax.dynamic_update_slice_in_dim(y_new, work_now, (big ^ it) * back, axis=0)
+    return y_new
 
 
 def normalize(owned_rows):
@@ -46,11 +62,7 @@
     own_offset = row_place * block_rows + cross_place * per_owner
     received = (
         lax.all_to_all(
-            lax.all_to_all(first_packed, "row", split_axis=0, concat_axis=0, tiled=True),
-            ("col", "rep"),
-            split_axis=1,
-            concat_axis=1,
-            tiled=True,
+            fix_digits(first_packed), ("col", "rep"), split_axis=1, concat_axis=1, tiled=True
         ),
         lax.all_to_all(
             lax.all_to_all(first_placed, "row", split_axis=0, concat_axis=0, tiled=True),

time: 93.1 us -> 86 us (0.924)
  waiting for transfers between devices: 22.7 us -> 13.2 us
  local copies, waits for them, and re-layouts: 13.7 us -> 15.7 us
  starting transfers between devices: 16.5 us -> 17.5 us
    all_to_all x2 -> x1, waiting for transfers between devices: 17.1 us -> 7.27 us  [body(): lax.all_to_all(fix_digits(first_packed), ('col', 'rep'), split_axis=1, co...]
    ppermute x0 -> x3, starting transfers between devices: none -> 5.68 us  [fix_digits(): lax.ppermute(work_now, 'row', list(map(lambda ii: (ii, ii ^ it), range(r1...]
    all_to_all x2 -> x1, starting transfers between devices: 6.92 us -> 3.46 us  [body(): lax.all_to_all(fix_digits(first_packed), ('col', 'rep'), split_axis=1, co...]
    dynamic_update_slice x0 -> x4, local copies, waits for them, and re-layouts: none -> 2.61 us  [fix_digits(): lax.dynamic_update_slice_in_dim(y_new, work_now, (big ^ it) * back, axis=0)]
    all_to_all x1, waiting for transfers between devices: 2.57 us -> 4.14 us  [body(): lax.all_to_all(first_placed, 'row', split_axis=0, concat_axis=0, tiled=True)]
    all_to_all x1, starting transfers between devices: 6.32 us -> 5.09 us  [body(): lax.all_to_all(first_placed, 'row', split_axis=0, concat_axis=0, tiled=True)]
    all_to_all x1, waiting for transfers between devices: 2.98 us -> 1.81 us  [body(): lax.all_to_all(lax.all_to_all(first_placed, 'row', split_axis=0, concat_a...]
  transfers between devices with their start and end apart: 4 -> 6, of which waited for: 4 -> 3; matrix products, arithmetic and copies ran while one was open for 5% -> 9% of each run, Pallas kernels for 0% -> 0%
where the time goes in v1:
time: 86 us; the launch traced here: 85.6 us
  blocking collectives  32.3 us (38%)
  starting transfers between devices  17.5 us (20%)
  local copies, waits for them, and re-layouts  15.7 us (18%)
  waiting for transfers between devices  13.2 us (15%)
  matrix products  2.52 us (3%)
  loops' own time  2.18 us (3%)
  other arithmetic  1.38 us (2%)
    all_gather x1, blocking collectives, body(): column_block = lax.all_gather(row_owned, 'row', axis=0, tiled=True)  17.5 us
    all_gather x1, blocking collectives, body(): row_block = lax.all_gather(row_owned, ('col', 'rep'), axis=0, tiled=True)  7.67 us
    all_to_all x1, waiting for transfers between devices, body(): lax.all_to_all(fix_digits(first_packed), ('col', 'rep'), split_axis=1, co...  7.27 us
    pmax x1, blocking collectives, body(): combined = lax.pmax(maxima, ('col', 'rep'))  7.06 us
    ppermute x3, starting transfers between devices, fix_digits(): lax.ppermute(work_now, 'row', list(map(lambda ii: (ii, ii ^ it), range(r1...  5.68 us
    all_to_all x1, starting transfers between devices, body(): lax.all_to_all(first_placed, 'row', split_axis=0, concat_axis=0, tiled=True)  5.09 us
    all_to_all x1, waiting for transfers between devices, body(): lax.all_to_all(first_placed, 'row', split_axis=0, concat_axis=0, tiled=True)  4.14 us
    all_to_all x1, starting transfers between devices, body(): lax.all_to_all(fix_digits(first_packed), ('col', 'rep'), split_axis=1, co...  3.46 us
  transfers between devices with their start and end apart: 6, of which 3 were waited for; matrix products, arithmetic and copies ran while one was open for 9% of the time, Pallas kernels for 0%

profile of v1, /device:TPU:0, one launch (start us, length us, event | category | flops | bytes accessed | tf_op | source)
XLA Modules:
  0.0 85.6 jit_solution(15909123457426097906)
XLA Ops:
  0.7 0.7 copy-done
  1.4 0.9 %reduce-window.6 = s32[16,3,128]{2,0,1:T(8,128)S(1)} reduce-window(s32[16,3,128]{2,0,1:T(8,128)S(1)} %copy_bitcast_fusion, s32[]{:T(128)} %constant.85.clone.1), window={size=1x1x128 pad=0_0x0_0x127_0}, to_apply=%region_0.1 | reduce-window | flops 780288 | bytes 49156 | tf_op jit(solution)/shard_map/reduce-window
  2.6 2.4 %scatter_custom_fusion.1 = bf16[384,512]{1,0:T(8,128)(2,1)S(1)} fusion(s32[360]{0:T(512)S(1)} %compare_select_fusion.1, bf16[360,512]{1,0:T(8,128)(2,1)} %param.5, bf16[]{:T(256)} %constant.87.clone.1), kind=kCustom, calls=%fused_computation.27 | custom fusion | bytes 393728 | tf_op jit(solution)/shard_map/scatter | solution.py:55
  5.1 3.1 %collective-permute-start = (bf16[1,4,24,512]{3,2,0,1:T(8,128)(2,1)S(1)}, bf16[1,4,24,512]{3,2,0,1:T(8,128)(2,1)S(1)}, u32[]{:S(2)}, u32[]{:S(2)}) collective-permute-start(bf16[1,4,24,512]{3,2,0,1:T(8,128)(2,1)S(1)} %get-tuple-element.111), channel_id=1, source_target_pairs={{0,4},{4,0},{8,12},{12,8},{1,5},{5,1},{9,13},{13,9},{2,6},{6,2},{1... | collective-permute-start | bytes 294920 | tf_op jit(solution)/shard_map/ppermute | solution.py:21
  8.2 2.6 %collective-permute-start.1 = (bf16[1,4,24,512]{3,2,0,1:T(8,128)(2,1)S(1)}, bf16[1,4,24,512]{3,2,0,1:T(8,128)(2,1)S(1)}, u32[]{:S(2)}, u32[]{:S(2)}) collective-permute-start(bf16[1,4,24,512]{3,2,0,1:T(8,128)(2,1)S(1)} %get-tuple-element.110), channel_id=1, source_target_pairs={{0,8},{4,12},{8,0},{12,4},{1,9},{5,13},{9,1},{13,5},{2,10},{6,14},... | collective-permute-start | bytes 294920 | tf_op jit(solution)/shard_map/ppermute | solution.py:21
  10.8 2.9 %scatter_custom_fusion = s32[384]{0:T(512)S(1)} fusion(s32[360]{0:T(512)S(1)} %compare_select_fusion.1, s32[360]{0:T(512)S(1)} %get-tuple-element.104, s32[]{:T(128)} %constant.88.clone.1), kind=kCustom, calls=%fused_computation.74 | custom fusion | bytes 1540 | tf_op jit(solution)/shard_map/scatter | solution.py:58
  13.7 0.7 reshape.115
  14.4 5.1 %all-to-all-start = ((s32[4,4,24]{2,1,0:T(4,128)}), s32[4,4,24]{2,1,0:T(4,128)S(1)}, u32[]{:S(2)}, u32[]{:S(2)}) async-start(s32[4,4,24]{2,1,0:T(4,128)} %reshape.115), calls=%async_computation | async-start | bytes 16384 | tf_op jit(solution)/shard_map/all_to_all | solution.py:68
  19.5 0.8 broadcast_in_dim.74
  20.3 0.7 bitcast_dynamic-update-slice_fusion
  20.9 4.1 %all-to-all-done = s32[4,4,24]{2,1,0:T(4,128)S(1)} async-done(((s32[4,4,24]{2,1,0:T(4,128)}), s32[4,4,24]{2,1,0:T(4,128)S(1)}, u32[]{:S(2)}, u32[]{:S(2)}) %all-to-all-start) | async-done | bytes 1568 | tf_op jit(solution)/shard_map/all_to_all | solution.py:68
  25.1 0.6 copy.14
  25.7 3.2 %all-to-all-start.1 = ((s32[4,4,24]{2,0,1:T(4,128)}), s32[4,4,24]{2,0,1:T(4,128)S(1)}, u32[]{:S(2)}, u32[]{:S(2)}) async-start(s32[4,4,24]{2,0,1:T(4,128)} %copy.14), calls=%async_computation.1 | async-start | bytes 16384 | tf_op jit(solution)/shard_map/all_to_all | solution.py:67
  28.9 0.7 constant_dynamic-update-slice_fusion.2
  29.6 0.6 constant_dynamic-update-slice_fusion.1
  30.2 0.6 constant_dynamic-update-slice_fusion
  30.9 1.8 %all-to-all-done.1 = s32[4,4,24]{2,0,1:T(4,128)S(1)} async-done(((s32[4,4,24]{2,0,1:T(4,128)}), s32[4,4,24]{2,0,1:T(4,128)S(1)}, u32[]{:S(2)}, u32[]{:S(2)}) %all-to-all-start.1) | async-done | bytes 1568 | tf_op jit(solution)/shard_map/all_to_all | solution.py:67
  32.7 3.5 %all-to-all-start.2 = ((bf16[4,4,24,512]{3,2,0,1:T(8,128)(2,1)}), bf16[4,4,24,512]{3,2,0,1:T(8,128)(2,1)S(1)}, u32[]{:S(2)}, u32[]{:S(2)}) async-start(bf16[4,4,24,512]{3,2,0,1:T(8,128)(2,1)} %constant_dynamic-update-slice_fusion), calls=%async_computation.2 | async-start | bytes 786432 | tf_op jit(solution)/shard_map/all_to_all | solution.py:64
  36.3 7.3 %all-to-all-done.2 = bf16[4,4,24,512]{3,2,0,1:T(8,128)(2,1)S(1)} async-done(((bf16[4,4,24,512]{3,2,0,1:T(8,128)(2,1)}), bf16[4,4,24,512]{3,2,0,1:T(8,128)(2,1)S(1)}, u32[]{:S(2)}, u32[]{:S(2)}) %all-to-all-start.2) | async-done | bytes 393248 | tf_op jit(solution)/shard_map/all_to_all | solution.py:64
  43.6 2.0 %scatter_custom_fusion.2 = bf16[192,512]{1,0:T(8,128)(2,1)S(1)} fusion(s32[384]{0:T(512)S(1)} %fusion.35, bf16[384,512]{1,0:T(8,128)(2,1)S(1)} %bitcast.50, bf16[]{:T(256)} %constant.87.clone.1), kind=kCustom, calls=%fused_computation.33 | custom fusion | bytes 196610 | tf_op jit(solution)/shard_map/scatter | solution.py:79
  45.8 17.5 %all_gather.7 = bf16[768,512]{1,0:T(8,128)(2,1)S(1)} all-gather(bf16[192,512]{1,0:T(8,128)(2,1)S(1)} %fusion.16), channel_id=1, replica_groups=mesh['grp'=2,'row'=4,'col'=2,'rep'=2] {'row'}, dimensions={0}, use_global_device_ids=true | all-gather | bytes 983040 | tf_op jit(solution)/shard_map/all_gather | solution.py:84
  63.4 7.7 %all_gather.6 = bf16[768,512]{1,0:T(8,128)(2,1)S(1)} all-gather(bf16[192,512]{1,0:T(8,128)(2,1)S(1)} %fusion.16), channel_id=1, replica_groups=mesh['grp'=2,'row'=4,'col'=2,'rep'=2] {'col','rep'}, dimensions={0}, use_global_device_ids=true | all-gather | bytes 983040 | tf_op jit(solution)/shard_map/all_gather | solution.py:82
  71.0 6.9 %while.12 = (s32[]{:T(128)}, f32[3,256]{1,0:T(4,128)S(1)}, s32[3]{0:T(128)S(1)}, s32[]{:T(128)}, s32[768]{0:T(1024)S(1)}, /*index=5*/bf16[3,256,512]{2,1,0:T(8,1...) while((s32[]{:T(128)}, f32[3,256]{1,0:T(4,128)S(1)}, s32[3]{0:T(128)S(1)}, s32[]{:T(128)}, ...), condition=%wide.region_11.12_spmd, body=%wide.region_7.11_spmd.sunk | while | flops 201916672 | bytes 1595529 | solution.py:108
  71.0 0.7 dynamic_slice.55
  72.4 0.3 fusion.58
  73.0 0.3 fusion.56
  73.3 0.7 dynamic_slice.55
  75.3 0.3 fusion.56
  75.6 0.7 dynamic_slice.55
  77.0 0.3 fusion.58
  77.9 7.1 %pmax.7 = f32[768]{0:T(1024)S(1)} all-reduce(f32[768]{0:T(1024)S(1)} %reshape.119), channel_id=1, replica_groups=mesh['grp'=2,'row'=4,'col'=2,'rep'=2] {'col','rep'}, use_global_device_ids=true, to_apply=%region_12.13 | all-reduce | flops 768 | bytes 6144 | tf_op jit(solution)/shard_map/pmax | solution.py:111
  85.0 0.6 dynamic_slice.31
  (41 shorter events, 2.4 us)
Async XLA Ops:
  0.7 0.7 copy-start
  5.1 23.8 %collective-permute-start = (bf16[1,4,24,512]{3,2,0,1:T(8,128)(2,1)S(1)}, bf16[1,4,24,512]{3,2,0,1:T(8,128)(2,1)S(1)}, u32[]{:S(2)}, u32[]{:S(2)}) collective-permute-start(bf16[1,4,24,512]{3,2,0,1:T(8,128)(2,1)S(1)} %get-tuple-element.111), channel_id=1, source_target_pairs={{0,4},{4,0},{8,12},{12,8},{1,5},{5,1},{9,13},{13,9},{2,6},{6,2},{1... | collective-permute-start | bytes 294920 | tf_op jit(solution)/shard_map/ppermute | solution.py:21
  8.2 21.4 %collective-permute-start.1 = (bf16[1,4,24,512]{3,2,0,1:T(8,128)(2,1)S(1)}, bf16[1,4,24,512]{3,2,0,1:T(8,128)(2,1)S(1)}, u32[]{:S(2)}, u32[]{:S(2)}) collective-permute-start(bf16[1,4,24,512]{3,2,0,1:T(8,128)(2,1)S(1)} %get-tuple-element.110), channel_id=1, source_target_pairs={{0,8},{4,12},{8,0},{12,4},{1,9},{5,13},{9,1},{13,5},{2,10},{6,14},... | collective-permute-start | bytes 294920 | tf_op jit(solution)/shard_map/ppermute | solution.py:21
  10.8 19.5 %collective-permute-start.2 = (bf16[1,4,24,512]{3,2,0,1:T(8,128)(2,1)S(1)}, bf16[1,4,24,512]{3,2,0,1:T(8,128)(2,1)S(1)}, u32[]{:S(2)}, u32[]{:S(2)}) collective-permute-start(bf16[1,4,24,512]{3,2,0,1:T(8,128)(2,1)S(1)} %get-tuple-element.109), channel_id=1, source_target_pairs={{0,12},{4,8},{8,4},{12,0},{1,13},{5,9},{9,5},{13,1},{2,14},{6,10},... | collective-permute-start | bytes 294920 | tf_op jit(solution)/shard_map/ppermute | solution.py:21
  14.4 10.7 %all-to-all-start = ((s32[4,4,24]{2,1,0:T(4,128)}), s32[4,4,24]{2,1,0:T(4,128)S(1)}, u32[]{:S(2)}, u32[]{:S(2)}) async-start(s32[4,4,24]{2,1,0:T(4,128)} %reshape.115), calls=%async_computation | async-start | bytes 16384 | tf_op jit(solution)/shard_map/all_to_all | solution.py:68
  25.7 7.0 %all-to-all-start.1 = ((s32[4,4,24]{2,0,1:T(4,128)}), s32[4,4,24]{2,0,1:T(4,128)S(1)}, u32[]{:S(2)}, u32[]{:S(2)}) async-start(s32[4,4,24]{2,0,1:T(4,128)} %copy.14), calls=%async_computation.1 | async-start | bytes 16384 | tf_op jit(solution)/shard_map/all_to_all | solution.py:67
  32.7 10.9 %all-to-all-start.2 = ((bf16[4,4,24,512]{3,2,0,1:T(8,128)(2,1)}), bf16[4,4,24,512]{3,2,0,1:T(8,128)(2,1)S(1)}, u32[]{:S(2)}, u32[]{:S(2)}) async-start(bf16[4,4,24,512]{3,2,0,1:T(8,128)(2,1)} %constant_dynamic-update-slice_fusion), calls=%async_computation.2 | async-start | bytes 786432 | tf_op jit(solution)/shard_map/all_to_all | solution.py:64
